TPU v7x, 32 devices: a whole 2x2x4 slice. The times are simulated.
32 devices in a mesh: tm: 4 (over y, x), freq: 8 (over z, core).
Axes of the slice: x: 2, y: 2, z: 4, core: 2. Of those that a mesh axis runs over, the one named last changes fastest.
Arguments:
- records: bfloat16 [1024, 512, 512], P('freq', 'tm'), may hold values from -4 to 4
- gap_flags: int32 [1024, 16], P('freq', 'tm'), may hold values from -2147483648 to 2147483647
- station_mask: int32 [1024], P('freq'), may hold values 0 or 1
Outputs:
- cross_spectra: float32 [16, 2, 1024, 1024], P('freq', None, 'tm')
All inputs are finite; a program needn't handle non-finite values. No bound on the sum of `station_mask` on one device may be relied on, other than what follows from the above.
Results may differ from a plain program's by a relative error of at most 0.0013.
Values may be sent and summed in bfloat16 or wider, within the bound.
No kernel may reach another device: no remote copies, remote signals or barrier semaphores. Data moves between devices by JAX's collectives and lax.ppermute only.
A program may use at most 128 MiB of HBM per device.

v0:
```python
import math
import jax
import jax.numpy as jnp
from jax import lax
from jax.sharding import PartitionSpec as P

BAND_DEV = 2
FLOOR = 0.25


def transform_table(length, bin_count):
    sample_ids = jnp.arange(length, dtype=jnp.int32)
    bin_ids = jnp.arange(bin_count, dtype=jnp.int32)
    phase_ids = bin_ids[:, None] * sample_ids[None, :] % length
    angles = phase_ids.astype(jnp.float32) * (2.0 * math.pi / length)
    window_taper = 0.5 - 0.5 * jnp.cos(sample_ids.astype(jnp.float32) * (2.0 * math.pi / length))
    factor = window_taper / math.sqrt(length)
    dft_table = jnp.concatenate([jnp.cos(angles) * factor, -jnp.sin(angles) * factor], axis=0)
    return dft_table.astype(jnp.bfloat16)


def unpack_flags(packed_words):
    shifts = jnp.arange(32, dtype=jnp.int32)
    bit_values = jnp.bitwise_and(
        jnp.right_shift(packed_words[:, :, None], shifts[None, None, :]), 1
    )
    return bit_values.reshape(packed_words.shape[0], packed_words.shape[1] * 32)


def whiten(records, band_bins):
    bin_count = band_bins + 4
    dft_table = transform_table(records.shape[-1], bin_count)
    spectrum = jnp.einsum("cl,swl->scw", dft_table, records, preferred_element_type=jnp.float32)
    real_part = spectrum[:, :bin_count]
    imag_part = spectrum[:, bin_count:]
    magnitude = jnp.sqrt(real_part * real_part + imag_part * imag_part)
    smooth = (
        magnitude[:, 0:band_bins]
        + magnitude[:, 1 : band_bins + 1]
        + magnitude[:, 2 : band_bins + 2]
        + magnitude[:, 3 : band_bins + 3]
        + magnitude[:, 4 : band_bins + 4]
    ) / 5.0
    factor = 1.0 / jnp.maximum(smooth, FLOOR)
    whitened = jnp.stack(
        [real_part[:, 2 : band_bins + 2] * factor, imag_part[:, 2 : band_bins + 2] * factor], axis=2
    )
    return whitened.astype(jnp.bfloat16)


def block_terms(left_side, right_side):
    count_rows, bin_count, _, win_count = left_side.shape
    right_rows = right_side.shape[0]
    direct_left = left_side.reshape(count_rows, bin_count, 2 * win_count)
    turned_left = jnp.concatenate([left_side[:, :, 1], -left_side[:, :, 0]], axis=2)
    direct_right = right_side.reshape(right_rows, bin_count, 2 * win_count)
    real_part = jnp.einsum(
        "ifx,jfx->ifj", direct_left, direct_right, preferred_element_type=jnp.float32
    )
    imag_part = jnp.einsum(
        "ifx,jfx->ifj", turned_left, direct_right, preferred_element_type=jnp.float32
    )
    return jnp.stack([real_part, imag_part], axis=2).reshape(count_rows, 2 * bin_count, right_rows)


def local(records, gap_flags, station_mask):
    freq_size = lax.axis_size("freq")
    time_size = lax.axis_size("tm")
    band_bins = BAND_DEV * freq_size
    whitened = whiten(records, band_bins)
    kept_words = gap_flags * station_mask[:, None]
    spectra = lax.all_to_all(whitened, "freq", split_axis=1, concat_axis=0, tiled=True)
    all_words = lax.all_gather(kept_words, "freq", axis=0, tiled=True)
    here_flags = unpack_flags(all_words).astype(jnp.bfloat16)
    masked = spectra * here_flags[:, None, None, :]
    stations = spectra.shape[0]
    row_count = stations // time_size
    row_start = lax.axis_index("tm") * row_count
    every_words = lax.all_gather(all_words, "tm", axis=1, tiled=True)
    every_flags = unpack_flags(every_words).astype(jnp.bfloat16)
    row_flags = lax.dynamic_slice_in_dim(every_flags, row_start, row_count, 0)
    counts = jnp.dot(row_flags, every_flags.T, preferred_element_type=jnp.float32)
    window_part = lax.all_gather(masked, "tm", axis=3, tiled=True)
    left_side = lax.dynamic_slice_in_dim(window_part, row_start, row_count, 0)
    stacks = block_terms(left_side, window_part)
    divisor = jnp.maximum(counts, 1.0)
    result = stacks / divisor[:, None, :]
    return result.reshape(row_count, BAND_DEV, 2, stations).transpose(1, 2, 0, 3)


def solution(mesh):
    placed = (P("freq", "tm", None), P("freq", "tm"), P("freq"))
    return jax.shard_map(
        local, mesh=mesh, in_specs=placed, out_specs=P("freq", None, "tm", None), check_vma=False
    )
```

profile of v0, /device:TPU:0, one launch (start us, length us, event | category | flops | bytes accessed | tf_op | source)
XLA Modules:
  0.0 130.0 jit_solution(13890323300610356222)
XLA Ops:
  6.6 0.2 multiply_convert_fusion.1
  6.8 8.5 %convolution_bitcast_fusion = f32[128,40,128]{2,1,0:T(8,128)S(1)} fusion(bf16[128,128,512]{2,1,0:T(8,128)(2,1)} %param.3, bf16[20,512]{1,0:T(8,128)(2,1)S(1)} %get-tuple-element.10, bf16[20,512]{1,0:T(8,128)(2,1)S(1)} %get-tuple-element.9), kind=kOutput, calls=%fused_computation.5 | convolution fusion | flops 671170560 | bytes 19439616 | tf_op jit(solution)/shard_map/cl,swl->scw/dot_general | solution.py:33
  15.3 0.6 fusion.4
  15.9 0.7 fusion.13
  16.6 0.2 fusion.14
  16.8 0.1 pad_maximum_fusion
  16.9 0.0 copy-start.1
  16.9 0.0 copy-start.2
  16.9 1.2 copy.17
  18.2 6.3 %all-to-all-start = ((bf16[128,16,2,128]{3,0,2,1:T(8,128)(2,1)}), bf16[128,16,2,128]{3,0,2,1:T(8,128)(2,1)S(1)}, u32[]{:S(2)}, u32[]{:S(2)}) async-start(bf16[128,16,2,128]{3,0,2,1:T(8,128)(2,1)} %copy.17), calls=%async_computation | async-start | bytes 2097152 | tf_op jit(solution)/shard_map/all_to_all | solution.py:72
  24.5 0.0 all-gather.3.cloned.1.call-start
  24.6 0.1 shift_right_arithmetic.47
  24.7 0.0 copy-done.1
  24.7 0.0 copy-done.2
  24.7 32.5 %all_gather.9 = s32[1024,4]{0,1:T(4,128)S(1)} all-gather(s32[128,4]{0,1:T(4,128)S(1)} %broadcast_multiply_fusion), channel_id=1, replica_groups=mesh['tm'=4,'freq'=8] {'freq'}, dimensions={0}, use_global_device_ids=true | all-gather | bytes 18432 | tf_op jit(solution)/shard_map/all_gather | solution.py:73
  57.2 0.1 fusion.17
  57.3 0.2 copy.19
  57.5 0.0 all-to-all-done
  57.5 0.1 copy.18
  57.6 1.1 bitcast_multiply_fusion
  58.7 0.0 all-gather.3.cloned.1.call-update
  58.8 0.1 shift_right_arithmetic.53
  58.8 8.2 %all-gather = s32[4,4,1024]{2,1,0:T(4,128)S(1)} all-gather(s32[1,4,1024]{2,1,0:T(4,128)S(1)} %bitcast.60), channel_id=1, replica_groups=mesh['tm'=4,'freq'=8] {'tm'}, dimensions={0}, use_global_device_ids=true | all-gather | bytes 81920 | tf_op jit(solution)/shard_map/all_gather | solution.py:79
  67.1 0.3 fusion.2
  67.4 0.5 convolution_maximum_fusion
  67.9 0.3 copy.22
  68.2 41.3 %all-gather.3.cloned.1.call-done = bf16[1024,2,2,512]{3,0,1,2:T(8,128)(2,1)} async-done(((bf16[1024,2,2,128]{3,0,1,2:T(8,128)(2,1)}), bf16[1024,2,2,512]{3,0,1,2:T(8,128)(2,1)}) %all-gather.3.cloned.1.call-update) | async-done | bytes 4194320 | tf_op jit(solution)/shard_map/all_gather | solution.py:83
  109.5 0.0 copy-start
  109.5 1.4 %dynamic-slice_bitcast_fusion = bf16[2,2,32,8,512]{4,3,2,1,0:T(8,128)(2,1)S(1)} fusion(bf16[1024,2,2,512]{3,0,1,2:T(8,128)(2,1)} %all-gather.3.cloned.1.call-done, s32[]{:T(128)S(6)} %select_n.14), kind=kLoop, calls=%fused_computation.29 | loop fusion | bytes 2097156
  111.0 0.1 copy.25
  111.1 0.9 copy-done
  112.1 0.6 copy.24
  112.7 1.3 %convolution_bitcast_fusion.2 = f32[256,2,1,1024]{0,3,1,2:T(8,128)S(1)} fusion(bf16[1024,2,1024]{2,0,1:T(8,128)(2,1)S(1)} %bitcast.54, bf16[256,2,1024]{2,0,1:T(8,128)(2,1)S(1)} %bitcast.57), kind=kOutput, calls=%fused_computation.7 | convolution fusion | flops 1073741824 | bytes 7340032 | tf_op jit(solution)/shard_map/ifx,jfx->ifj/dot_general | solution.py:57
  114.0 0.1 dynamic-slice_bitcast_fusion.1
  114.1 1.3 %convolution_bitcast_fusion.1 = f32[256,2,1,1024]{0,3,1,2:T(8,128)S(1)} fusion(bf16[1024,2,1024]{2,0,1:T(8,128)(2,1)S(1)} %bitcast.55, bf16[256,2,512]{2,0,1:T(8,128)(2,1)S(1)} %get-tuple-element.8, bf16[256,2,512]{2,0,1:T(8,128)(2,1)S(1)} %get-tuple-element.7), kind=kOutput, calls=%fused_computation.6 | convolution fusion | flops 1075838976 | bytes 7340032 | tf_op jit(solution)/shard_map/ifx,jfx->ifj/dot_general | solution.py:60
  115.5 2.3 %fusion = f32[2,2,256,1024]{2,3,0,1:T(8,128)} fusion(f32[256,2,1,1024]{0,3,1,2:T(8,128)S(1)} %convolution_bitcast_fusion.1, f32[256,2,1,1024]{0,3,1,2:T(8,128)S(1)} %convolution_bitcast_fusion.2, f32[256,1024]{0,1:T(8,128)S(1)} %copy.22), kind=kLoop, calls=%fused_computation.1 | loop fusion | flops 2097152 | bytes 9437184 | tf_op jit(solution)/shard_map/transpose | solution.py:88
  117.8 5.3 %copy.23 = f32[2,2,256,1024]{3,2,1,0:T(8,128)} copy(f32[2,2,256,1024]{2,3,0,1:T(8,128)} %fusion) | data formatting | bytes 8388608 | tf_op jit(solution)/shard_map/transpose | solution.py:88
  (5 shorter events, 0.1 us)
Async XLA Ops:
  16.9 7.8 %copy-start.1 = (s32[128,4]{0,1:T(4,128)S(1)}, s32[128,4]{0,1:T(4,128)}, u32[]{:S(2)}) copy-start(s32[128,4]{0,1:T(4,128)} %param.4) | copy-start | bytes 6148
  16.9 7.7 %copy-start.2 = (s32[128]{0:T(128)S(1)}, s32[128]{0:T(128)}, u32[]{:S(2)}) copy-start(s32[128]{0:T(128)} %param.5) | copy-start | bytes 1540
  18.2 39.3 %all-to-all-start = ((bf16[128,16,2,128]{3,0,2,1:T(8,128)(2,1)}), bf16[128,16,2,128]{3,0,2,1:T(8,128)(2,1)S(1)}, u32[]{:S(2)}, u32[]{:S(2)}) async-start(bf16[128,16,2,128]{3,0,2,1:T(8,128)(2,1)} %copy.17), calls=%async_computation | async-start | bytes 2097152 | tf_op jit(solution)/shard_map/all_to_all | solution.py:72
  24.5 85.0 %all-gather.3.cloned.1.call-start = ((), (), s32[]{:S(2)}) async-start(), calls=%async_computation.1 | async-start | bytes 5242880 | tf_op jit(solution)/shard_map/all_gather | solution.py:83
  109.5 2.5 %copy-start = (bf16[1024,2,2,512]{3,0,1,2:T(8,128)(2,1)S(1)}, bf16[1024,2,2,512]{3,0,1,2:T(8,128)(2,1)}, u32[]{:S(2)}) copy-start(bf16[1024,2,2,512]{3,0,1,2:T(8,128)(2,1)} %all-gather.3.cloned.1.call-done) | copy-start | bytes 12582916
Sparse Core Ops, SparseCore 0:
  58.9 50.6 all-gather.2
where the time goes:
time: 130 us
  waiting for transfers between devices  41.3 us (32%)
  blocking collectives  40.7 us (31%)
  between operations  13.6 us (10%)
  matrix products  11.6 us (9%)
  local copies, waits for them, and re-layouts  10.5 us (8%)
  starting transfers between devices  6.38 us (5%)
  other arithmetic  5.85 us (4%)
    all_gather x1, waiting for transfers between devices, local(): window_part = lax.all_gather(masked, 'tm', axis=3, tiled=True)  41.3 us
    all_gather x1, blocking collectives, local(): all_words = lax.all_gather(kept_words, 'freq', axis=0, tiled=True)  32.5 us
    dot_general x1, matrix products, whiten(): jnp.einsum('cl,swl->scw', dft_table, records, preferred_element_type=jnp....  8.47 us
    all_gather x1, blocking collectives, local(): every_words = lax.all_gather(all_words, 'tm', axis=1, tiled=True)  8.24 us
    all_to_all x1, starting transfers between devices, local(): lax.all_to_all(whitened, 'freq', split_axis=1, concat_axis=0, tiled=True)  6.35 us
    transpose x1, local copies, waits for them, and re-layouts, local(): result.reshape(row_count, BAND_DEV, 2, stations).transpose(1, 2, 0, 3)  5.34 us
  transfers between devices with their start and end apart: 2, of which 1 were waited for; matrix products, arithmetic and copies ran while one was open for 1% of the time, Pallas kernels for 0%

commit v1 on v0

--- a/solution.py
+++ b/solution.py
@@ -6,6 +6,18 @@
 
 BAND_DEV = 2
 FLOOR = 0.25
+
+
+def gather_by_bits(array, axis, dim):
+    ways, here = (lax.axis_size(axis), lax.axis_index(axis))
+    grown, reach = (array, 1)
+    while reach < ways:
+        theirs = lax.ppermute(grown, axis, [(d, d ^ reach) for d in range(ways)])
+        mine_first = jnp.concatenate([grown, theirs], axis=dim)
+        theirs_first = jnp.concatenate([theirs, grown], axis=dim)
+        grown = jnp.where(here & reach == 0, mine_first, theirs_first)
+        reach = 2 * reach
+    return grown
 
 
 def transform_table(length, bin_count):
@@ -70,7 +82,7 @@
     whitened = whiten(records, band_bins)
     kept_words = gap_flags * station_mask[:, None]
     spectra = lax.all_to_all(whitened, "freq", split_axis=1, concat_axis=0, tiled=True)
-    all_words = lax.all_gather(kept_words, "freq", axis=0, tiled=True)
+    all_words = gather_by_bits(kept_words, "freq", 0)
     here_flags = unpack_flags(all_words).astype(jnp.bfloat16)
     masked = spectra * here_flags[:, None, None, :]
     stations = spectra.shape[0]

time: 130 us -> 125 us (0.962)
  blocking collectives: 40.7 us -> 8.24 us
  waiting for transfers between devices: 41.3 us -> 62.1 us
  starting transfers between devices: 6.38 us -> 13.1 us
    all_gather x1 -> x0, blocking collectives: 32.5 us -> none  [local(): all_words = lax.all_gather(kept_words, 'freq', axis=0, tiled=True)]
    ppermute x0 -> x3, waiting for transfers between devices: none -> 20 us  [gather_by_bits(): theirs = lax.ppermute(grown, axis, [(d, d ^ reach) for d in range(ways)])]
    ppermute x0 -> x3, starting transfers between devices: none -> 6.69 us  [gather_by_bits(): theirs = lax.ppermute(grown, axis, [(d, d ^ reach) for d in range(ways)])]
  transfers between devices with their start and end apart: 2 -> 5, of which waited for: 1 -> 4; matrix products, arithmetic and copies ran while one was open for 1% -> 1% of each run, Pallas kernels for 0% -> 0%
where the time goes in v1:
time: 125 us
  waiting for transfers between devices  62.1 us (50%)
  between operations  13.6 us (11%)
  starting transfers between devices  13.1 us (10%)
  matrix products  11.6 us (9%)
  local copies, waits for them, and re-layouts  10.5 us (8%)
  blocking collectives  8.24 us (7%)
  other arithmetic  5.86 us (5%)
    all_gather x1, waiting for transfers between devices, local(): window_part = lax.all_gather(masked, 'tm', axis=3, tiled=True)  42.1 us
    ppermute x3, waiting for transfers between devices, gather_by_bits(): theirs = lax.ppermute(grown, axis, [(d, d ^ reach) for d in range(ways)])  20 us
    dot_general x1, matrix products, whiten(): jnp.einsum('cl,swl->scw', dft_table, records, preferred_element_type=jnp....  8.47 us
    all_gather x1, blocking collectives, local(): every_words = lax.all_gather(all_words, 'tm', axis=1, tiled=True)  8.24 us
    ppermute x3, starting transfers between devices, gather_by_bits(): theirs = lax.ppermute(grown, axis, [(d, d ^ reach) for d in range(ways)])  6.69 us
    all_to_all x1, starting transfers between devices, local(): lax.all_to_all(whitened, 'freq', split_axis=1, concat_axis=0, tiled=True)  6.35 us
    transpose x1, local copies, waits for them, and re-layouts, local(): result.reshape(row_count, BAND_DEV, 2, stations).transpose(1, 2, 0, 3)  5.34 us
  transfers between devices with their start and end apart: 5, of which 4 were waited for; matrix products, arithmetic and copies ran while one was open for 1% of the time, Pallas kernels for 0%

profile of v1, /device:TPU:0, one launch (start us, length us, event | category | flops | bytes accessed | tf_op | source)
XLA Modules:
  0.0 125.0 jit_solution(11087243314948961774)
XLA Ops:
  6.6 0.2 multiply_convert_fusion.1
  6.8 8.5 %convolution_bitcast_fusion = f32[128,40,128]{2,1,0:T(8,128)S(1)} fusion(bf16[128,128,512]{2,1,0:T(8,128)(2,1)} %param.3, bf16[20,512]{1,0:T(8,128)(2,1)S(1)} %get-tuple-element.10, bf16[20,512]{1,0:T(8,128)(2,1)S(1)} %get-tuple-element.9), kind=kOutput, calls=%fused_computation.5 | convolution fusion | flops 671170560 | bytes 19439616 | tf_op jit(solution)/shard_map/cl,swl->scw/dot_general | solution.py:45
  15.3 0.6 fusion.4
  15.9 0.7 fusion.13
  16.6 0.2 fusion.14
  16.8 0.1 pad_maximum_fusion
  16.9 0.0 copy-start.1
  16.9 0.0 copy-start.2
  16.9 1.2 copy.17
  18.2 6.3 %all-to-all-start = ((bf16[128,16,2,128]{3,0,2,1:T(8,128)(2,1)}), bf16[128,16,2,128]{3,0,2,1:T(8,128)(2,1)S(1)}, u32[]{:S(2)}, u32[]{:S(2)}) async-start(bf16[128,16,2,128]{3,0,2,1:T(8,128)(2,1)} %copy.17), calls=%async_computation | async-start | bytes 2097152 | tf_op jit(solution)/shard_map/all_to_all | solution.py:84
  24.5 0.0 all-gather.3.cloned.1.call-start
  24.6 0.0 copy-done.1
  24.6 0.0 copy-done.2
  24.6 0.5 collective-permute-start
  25.1 1.0 collective-permute-done
  26.1 1.7 %collective-permute-start.1 = (s32[256,4]{0,1:T(4,128)S(1)}, s32[256,4]{0,1:T(4,128)S(1)}, u32[]{:S(2)}, u32[]{:S(2)}) collective-permute-start(s32[256,4]{0,1:T(4,128)S(1)} %add_select_fusion.3), channel_id=1, source_target_pairs={{0,2},{1,3},{2,0},{3,1},{4,6},{5,7},{6,4},{7,5},{8,10},{9,11},{10,... | collective-permute-start | bytes 12296 | tf_op jit(solution)/shard_map/ppermute | solution.py:15
  27.8 14.9 %collective-permute-done.1 = s32[256,4]{0,1:T(4,128)S(1)} collective-permute-done((s32[256,4]{0,1:T(4,128)S(1)}, s32[256,4]{0,1:T(4,128)S(1)}, u32[]{:S(2)}, u32[]{:S(2)}) %collective-permute-start.1) | collective-permute-done | bytes 4128 | tf_op jit(solution)/shard_map/ppermute | solution.py:15
  42.7 4.4 %collective-permute-start.2 = (s32[512,4]{0,1:T(4,128)S(1)}, s32[512,4]{0,1:T(4,128)S(1)}, u32[]{:S(2)}, u32[]{:S(2)}) collective-permute-start(s32[512,4]{0,1:T(4,128)S(1)} %add_select_fusion.2), channel_id=1, source_target_pairs={{0,4},{1,5},{2,6},{3,7},{4,0},{5,1},{6,2},{7,3},{8,12},{9,13},{10,... | collective-permute-start | bytes 24584 | tf_op jit(solution)/shard_map/ppermute | solution.py:15
  47.1 0.1 shift_right_arithmetic.47
  47.2 4.2 %collective-permute-done.2 = s32[512,4]{0,1:T(4,128)S(1)} collective-permute-done((s32[512,4]{0,1:T(4,128)S(1)}, s32[512,4]{0,1:T(4,128)S(1)}, u32[]{:S(2)}, u32[]{:S(2)}) %collective-permute-start.2) | collective-permute-done | bytes 8224 | tf_op jit(solution)/shard_map/ppermute | solution.py:15
  51.4 0.1 fusion.17
  51.6 0.2 copy.19
  51.8 0.0 all-to-all-done
  51.8 0.1 copy.18
  51.8 1.1 bitcast_multiply_fusion
  53.0 0.0 all-gather.3.cloned.1.call-update
  53.0 0.1 shift_right_arithmetic.53
  53.1 8.2 %all-gather = s32[4,4,1024]{2,1,0:T(4,128)S(1)} all-gather(s32[1,4,1024]{2,1,0:T(4,128)S(1)} %bitcast.60), channel_id=1, replica_groups=mesh['tm'=4,'freq'=8] {'tm'}, dimensions={0}, use_global_device_ids=true | all-gather | bytes 81920 | tf_op jit(solution)/shard_map/all_gather | solution.py:91
  61.4 0.3 fusion.2
  61.7 0.5 convolution_maximum_fusion
  62.2 0.3 copy.22
  62.5 42.1 %all-gather.3.cloned.1.call-done = bf16[1024,2,2,512]{3,0,1,2:T(8,128)(2,1)} async-done(((bf16[1024,2,2,128]{3,0,1,2:T(8,128)(2,1)}), bf16[1024,2,2,512]{3,0,1,2:T(8,128)(2,1)}) %all-gather.3.cloned.1.call-update) | async-done | bytes 4194320 | tf_op jit(solution)/shard_map/all_gather | solution.py:95
  104.6 0.0 copy-start
  104.6 1.4 %dynamic-slice_bitcast_fusion = bf16[2,2,32,8,512]{4,3,2,1,0:T(8,128)(2,1)S(1)} fusion(bf16[1024,2,2,512]{3,0,1,2:T(8,128)(2,1)} %all-gather.3.cloned.1.call-done, s32[]{:T(128)S(6)} %select_n.51), kind=kLoop, calls=%fused_computation.29 | loop fusion | bytes 2097156
  106.0 0.1 copy.25
  106.2 0.9 copy-done
  107.1 0.6 copy.24
  107.7 1.3 %convolution_bitcast_fusion.2 = f32[256,2,1,1024]{0,3,1,2:T(8,128)S(1)} fusion(bf16[1024,2,1024]{2,0,1:T(8,128)(2,1)S(1)} %bitcast.54, bf16[256,2,1024]{2,0,1:T(8,128)(2,1)S(1)} %bitcast.57), kind=kOutput, calls=%fused_computation.7 | convolution fusion | flops 1073741824 | bytes 7340032 | tf_op jit(solution)/shard_map/ifx,jfx->ifj/dot_general | solution.py:69
  109.0 0.1 dynamic-slice_bitcast_fusion.1
  109.2 1.3 %convolution_bitcast_fusion.1 = f32[256,2,1,1024]{0,3,1,2:T(8,128)S(1)} fusion(bf16[1024,2,1024]{2,0,1:T(8,128)(2,1)S(1)} %bitcast.55, bf16[256,2,512]{2,0,1:T(8,128)(2,1)S(1)} %get-tuple-element.8, bf16[256,2,512]{2,0,1:T(8,128)(2,1)S(1)} %get-tuple-element.7), kind=kOutput, calls=%fused_computation.6 | convolution fusion | flops 1075838976 | bytes 7340032 | tf_op jit(solution)/shard_map/ifx,jfx->ifj/dot_general | solution.py:72
  110.5 2.3 %fusion = f32[2,2,256,1024]{2,3,0,1:T(8,128)} fusion(f32[256,2,1,1024]{0,3,1,2:T(8,128)S(1)} %convolution_bitcast_fusion.1, f32[256,2,1,1024]{0,3,1,2:T(8,128)S(1)} %convolution_bitcast_fusion.2, f32[256,1024]{0,1:T(8,128)S(1)} %copy.22), kind=kLoop, calls=%fused_computation.1 | loop fusion | flops 2097152 | bytes 9437184 | tf_op jit(solution)/shard_map/transpose | solution.py:100
  112.8 5.3 %copy.23 = f32[2,2,256,1024]{3,2,1,0:T(8,128)} copy(f32[2,2,256,1024]{2,3,0,1:T(8,128)} %fusion) | data formatting | bytes 8388608 | tf_op jit(solution)/shard_map/transpose | solution.py:100
  (8 shorter events, 0.1 us)
Async XLA Ops:
  16.9 7.7 %copy-start.1 = (s32[128,4]{0,1:T(4,128)S(1)}, s32[128,4]{0,1:T(4,128)}, u32[]{:S(2)}) copy-start(s32[128,4]{0,1:T(4,128)} %param.4) | copy-start | bytes 6148
  16.9 7.7 %copy-start.2 = (s32[128]{0:T(128)S(1)}, s32[128]{0:T(128)}, u32[]{:S(2)}) copy-start(s32[128]{0:T(128)} %param.5) | copy-start | bytes 1540
  18.2 33.6 %all-to-all-start = ((bf16[128,16,2,128]{3,0,2,1:T(8,128)(2,1)}), bf16[128,16,2,128]{3,0,2,1:T(8,128)(2,1)S(1)}, u32[]{:S(2)}, u32[]{:S(2)}) async-start(bf16[128,16,2,128]{3,0,2,1:T(8,128)(2,1)} %copy.17), calls=%async_computation | async-start | bytes 2097152 | tf_op jit(solution)/shard_map/all_to_all | solution.py:84
  24.5 80.0 %all-gather.3.cloned.1.call-start = ((), (), s32[]{:S(2)}) async-start(), calls=%async_computation.1 | async-start | bytes 5242880 | tf_op jit(solution)/shard_map/all_gather | solution.py:95
  24.6 1.5 %collective-permute-start = (s32[128,4]{0,1:T(4,128)S(1)}, s32[128,4]{0,1:T(4,128)S(1)}, u32[]{:S(2)}, u32[]{:S(2)}) collective-permute-start(s32[128,4]{0,1:T(4,128)S(1)} %broadcast_multiply_fusion), channel_id=1, source_target_pairs={{0,1},{1,0},{2,3},{3,2},{4,5},{5,4},{6,7},{7,6},{8,9},{9,8},{10,11... | collective-permute-start | bytes 6152 | tf_op jit(solution)/shard_map/ppermute | solution.py:15
  26.1 16.6 %collective-permute-start.1 = (s32[256,4]{0,1:T(4,128)S(1)}, s32[256,4]{0,1:T(4,128)S(1)}, u32[]{:S(2)}, u32[]{:S(2)}) collective-permute-start(s32[256,4]{0,1:T(4,128)S(1)} %add_select_fusion.3), channel_id=1, source_target_pairs={{0,2},{1,3},{2,0},{3,1},{4,6},{5,7},{6,4},{7,5},{8,10},{9,11},{10,... | collective-permute-start | bytes 12296 | tf_op jit(solution)/shard_map/ppermute | solution.py:15
  42.7 8.8 %collective-permute-start.2 = (s32[512,4]{0,1:T(4,128)S(1)}, s32[512,4]{0,1:T(4,128)S(1)}, u32[]{:S(2)}, u32[]{:S(2)}) collective-permute-start(s32[512,4]{0,1:T(4,128)S(1)} %add_select_fusion.2), channel_id=1, source_target_pairs={{0,4},{1,5},{2,6},{3,7},{4,0},{5,1},{6,2},{7,3},{8,12},{9,13},{10,... | collective-permute-start | bytes 24584 | tf_op jit(solution)/shard_map/ppermute | solution.py:15
  104.6 2.5 %copy-start = (bf16[1024,2,2,512]{3,0,1,2:T(8,128)(2,1)S(1)}, bf16[1024,2,2,512]{3,0,1,2:T(8,128)(2,1)}, u32[]{:S(2)}) copy-start(bf16[1024,2,2,512]{3,0,1,2:T(8,128)(2,1)} %all-gather.3.cloned.1.call-done) | copy-start | bytes 12582916
Sparse Core Ops, SparseCore 0:
  53.1 51.4 all-gather.2
